TPU v7x, 256 devices: a whole 4x4x8 slice. The times are simulated.
256 devices in a mesh: trow: 16 (over x, y), tcol: 8 (over z), rep: 2 (over core).
Axes of the slice: x: 4, y: 4, z: 8, core: 2. Of those that a mesh axis runs over, the one named last changes fastest.
Arguments:
- users: float32 [131072, 128], P(('trow', 'tcol'))
- items: float32 [65536, 128], P(('tcol', 'trow'))
- ratings: bfloat16 [16, 8, 2, 64, 128, 128], P('trow', 'tcol', 'rep'), may hold values from -6 to 6
- row_mask: int32 [16, 8, 2, 64, 128], P('trow', 'tcol', 'rep'), may hold values 0 or 1
- col_mask: int32 [16, 8, 2, 64, 128], P('trow', 'tcol', 'rep'), may hold values 0 or 1
- row_slots: int32 [16, 8, 2, 64], P('trow', 'tcol', 'rep'), may hold values from 0 to 31, as said below
- col_slots: int32 [16, 8, 2, 64], P('trow', 'tcol', 'rep'), may hold values from 0 to 31, as said below
- send_users: int32 [16, 8, 2, 8, 4], P('trow', 'tcol', 'rep'), may hold values from 0 to 7, as said below
- send_items: int32 [16, 8, 2, 16, 2], P('trow', 'tcol', 'rep'), may hold values from 0 to 3, as said below
Outputs:
- users_out: float32 [131072, 128], P(('trow', 'tcol'))
- items_out: float32 [65536, 128], P(('tcol', 'trow'))
Inputs may be any that keep to these rules, and one draw needn't show every extreme that they name: `send_users`: distinct within each row of the last dimension. `send_items`: distinct within each row of the last dimension. `row_slots`: every slot is named by some tile of each device. `col_slots`: every slot is named by some tile of each device.
All inputs are finite; a program needn't handle non-finite values. No bound on the sum of `row_mask` or of `col_mask` on one device may be relied on, other than what follows from the above.
Results may differ from a plain program's by a relative error of at most 0.02.
Values may be sent and summed in bfloat16 or wider, within the bound.
A program may use at most 64 MiB of HBM per device.

v0:
```python
import jax
import jax.numpy as jnp
from jax import lax
from jax.sharding import PartitionSpec as P

ITERS = 2


def precondition(gradient, gramian):
    factor = jnp.linalg.cholesky(gramian)
    return jax.scipy.linalg.cho_solve((factor, True), gradient.T).T


def pool_sum(index_list, terms, pool_count):
    onehot = (
        lax.broadcasted_iota(jnp.int32, (pool_count, index_list.shape[0]), 0) == index_list[None, :]
    ).astype(jnp.bfloat16)
    flat = terms.reshape(terms.shape[0], -1)
    upper = flat.astype(jnp.bfloat16)
    lower = (flat - upper.astype(jnp.float32)).astype(jnp.bfloat16)
    return jnp.dot(onehot, upper, preferred_element_type=jnp.float32) + jnp.dot(
        onehot, lower, preferred_element_type=jnp.float32
    )


def on_device(
    users, items, ratings, row_mask, col_mask, row_slots, col_slots, send_users, send_items
):
    n_trow = lax.axis_size("trow")
    n_tcol = lax.axis_size("tcol")
    n_rep = lax.axis_size("rep")
    tile_size = ratings.shape[-1]
    rank_width = users.shape[1]
    tile_count = ratings.shape[3]
    own_users = users.shape[0] // tile_size
    own_items = items.shape[0] // tile_size
    user_cap = send_users.shape[-1]
    item_cap = send_items.shape[-1]
    ratings_local = ratings.reshape(tile_count, tile_size, tile_size)
    weights = (
        row_mask.reshape(tile_count, tile_size)[:, :, None]
        * col_mask.reshape(tile_count, tile_size)[:, None, :]
    ).astype(jnp.float32)
    row_slot_list = row_slots.reshape(-1)
    col_slot_list = col_slots.reshape(-1)
    user_sends = send_users.reshape(n_tcol, -1)
    item_sends = send_items.reshape(n_trow, -1)
    user_received = lax.all_to_all(
        user_sends, "tcol", split_axis=0, concat_axis=0, tiled=True
    ).reshape(-1)
    item_received = lax.all_to_all(
        item_sends, "trow", split_axis=0, concat_axis=0, tiled=True
    ).reshape(-1)
    row_list = row_slot_list // user_cap * own_users + user_received[row_slot_list]
    col_list = col_slot_list // item_cap * own_items + item_received[col_slot_list]
    all_users = own_users * tile_size * n_trow * n_tcol
    all_items = own_items * tile_size * n_trow * n_tcol
    user_coef = 2.0 * all_items * own_users / (tile_size * tile_count * n_rep)
    item_coef = 2.0 * all_users * own_items / (tile_size * tile_count * n_rep)
    for iteration in range(ITERS):
        gram_users, gram_items = lax.psum(
            (
                jnp.dot(
                    users.T,
                    users,
                    precision=lax.Precision.HIGHEST,
                    preferred_element_type=jnp.float32,
                ),
                jnp.dot(
                    items.T,
                    items,
                    precision=lax.Precision.HIGHEST,
                    preferred_element_type=jnp.float32,
                ),
            ),
            ("trow", "tcol"),
        )
        user_half = users.astype(jnp.bfloat16).reshape(own_users, tile_size, rank_width)
        item_half = items.astype(jnp.bfloat16).reshape(own_items, tile_size, rank_width)
        user_pool = lax.all_gather(user_half, "tcol", axis=0, tiled=True)
        item_pool = lax.all_gather(item_half, "trow", axis=0, tiled=True)
        x_tiles = user_pool[row_list]
        y_tiles = item_pool[col_list]
        predicted = jnp.einsum("tar,tbr->tab", x_tiles, y_tiles, preferred_element_type=jnp.float32)
        errors = (weights * (predicted - ratings_local.astype(jnp.float32))).astype(jnp.bfloat16)
        user_terms = jnp.einsum("tab,tbr->tar", errors, y_tiles, preferred_element_type=jnp.float32)
        item_terms = jnp.einsum("tab,tar->tbr", errors, x_tiles, preferred_element_type=jnp.float32)
        user_pooled = pool_sum(row_list, user_terms, user_pool.shape[0])
        item_pooled = pool_sum(col_list, item_terms, item_pool.shape[0])
        user_grad = lax.psum_scatter(user_pooled, "tcol", scatter_dimension=0, tiled=True)
        item_grad = lax.psum_scatter(item_pooled, "trow", scatter_dimension=0, tiled=True)
        user_grad, item_grad = lax.psum((user_grad, item_grad), "rep")
        new_users = users - user_coef * precondition(user_grad.reshape(-1, rank_width), gram_items)
        new_items = items - item_coef * precondition(item_grad.reshape(-1, rank_width), gram_users)
        users, items = (new_users, new_items)
    return (users, items)


def solution(mesh):
    return jax.shard_map(
        on_device,
        mesh=mesh,
        in_specs=(
            P(("trow", "tcol"), None),
            P(("tcol", "trow"), None),
            P("trow", "tcol", "rep", None, None, None),
            P("trow", "tcol", "rep", None, None),
            P("trow", "tcol", "rep", None, None),
            P("trow", "tcol", "rep", None),
            P("trow", "tcol", "rep", None),
            P("trow", "tcol", "rep", None, None),
            P("trow", "tcol", "rep", None, None),
        ),
        out_specs=(P(("trow", "tcol"), None), P(("tcol", "trow"), None)),
        check_vma=False,
    )
```

profile of v0, /device:TPU:1, one launch (start us, length us, event | category | flops | bytes accessed | tf_op | source)
XLA Modules:
  0.0 1075.5 jit_solution(2654260133140196737)
XLA Ops:
  7.2 1.8 convert_element_type.69
  9.1 1.6 convert_element_type.70
  10.7 1.3 copy.48
  12.1 7.6 all-to-all-start.1
  21.0 1.3 copy.47
  22.3 3.7 all-to-all-done.1
  26.1 8.2 all-to-all-start
  36.4 4.4 all-to-all-done
  42.3 9.4 all-gather.5.cloned.1.call-done
  51.7 3.7 gather_fusion.1
  55.4 50.8 %all-gather.7.cloned.1.call-done = bf16[64,128,128]{2,1,0:T(8,128)(2,1)} async-done(((bf16[4,128,128]{2,1,0:T(8,128)(2,1)}), bf16[64,128,128]{2,1,0:T(8,128)(2,1)}) %all-gather.7.cloned.1.call-update) | async-done | bytes 2097168 | tf_op jit(solution)/shard_map/all_gather | solution.py:81
  106.3 2.5 gather_fusion.3
  108.9 4.1 fusion.1
  113.0 0.9 fusion.61
  114.4 2.8 fusion.9
  117.2 4.9 convolution_add_fusion.2
  122.3 2.3 fusion.59
  124.6 2.8 fusion.8
  127.4 4.9 convolution_add_fusion.3
  132.4 0.9 copy-done.5
  133.2 1.2 fusion.58
  134.5 1.6 fusion.60
  137.4 98.5 %all-reduce.13.cloned.1.call-done = f32[64,16384]{1,0:T(8,128)} async-done(((f32[64,16384]{1,0:T(8,128)}), f32[64,16384]{1,0:T(8,128)}) %all-reduce.13.cloned.1.call-update) | async-done | bytes 4194320
  235.9 1.1 constant_dynamic-slice_fusion.1
  237.0 0.9 reshape.383
  237.9 55.8 %reduce-scatter.3.cloned.1.call-done = f32[8,16384]{1,0:T(8,128)} async-done(((f32[64,16384]{1,0:T(8,128)}), f32[8,16384]{1,0:T(8,128)}) %reduce-scatter.3.cloned.1.call-update) | async-done | bytes 524304 | tf_op jit(solution)/shard_map/reduce_scatter | solution.py:90
  293.7 1.9 reshape.380
  296.1 209.1 %all-reduce.19.cloned.1.call-done = (f32[128,128]{0,1:T(8,128)}, f32[128,128]{0,1:T(8,128)}) async-done(((f32[128,128]{0,1:T(8,128)}, f32[128,128]{0,1:T(8,128)}), (f32[128,128]{0,1:T(8,128)}, f32[128,128]{0,1:T(8,128)})) %all-reduce.19.cloned.1.call-update) | async-done | bytes 131088 | tf_op jit(solution)/shard_map/psum | solution.py:61
  505.3 0.9 copy.51
  506.2 0.9 copy.46
  507.1 0.9 fusion.39
  508.0 11.7 %cholesky.74 = f32[128,128]{1,0:T(8,128)S(1)} custom-call(f32[128,128]{1,0:T(8,128)S(1)} %get-tuple-element.24), custom_call_target="Cholesky" | custom-call | tf_op jit(solution)/shard_map/jit(cholesky)/cholesky | solution.py:10
  521.1 9.8 custom-call.14
  530.9 10.3 all-reduce.23.cloned.1.call-done
  541.2 1.7 fusion.41
  545.1 11.7 %cholesky.85 = f32[128,128]{1,0:T(8,128)S(1)} custom-call(f32[128,128]{1,0:T(8,128)S(1)} %get-tuple-element.23), custom_call_target="Cholesky" | custom-call | tf_op jit(solution)/shard_map/jit(cholesky)/cholesky | solution.py:10
  558.1 9.8 custom-call.15
  569.6 1.0 fusion.62
  570.6 1.2 fusion.64
  572.0 10.9 %all-gather.9.cloned.1.call-done = bf16[64,128,128]{2,1,0:T(8,128)(2,1)} async-done(((bf16[8,128,128]{2,1,0:T(8,128)(2,1)}), bf16[64,128,128]{2,1,0:T(8,128)(2,1)}) %all-gather.9.cloned.1.call-update) | async-done | bytes 2097168 | tf_op jit(solution)/shard_map/all_gather | solution.py:80
  582.9 3.7 gather_fusion.4
  586.7 50.5 %all-gather.11.cloned.1.call-done = bf16[64,128,128]{2,1,0:T(8,128)(2,1)} async-done(((bf16[4,128,128]{2,1,0:T(8,128)(2,1)}), bf16[64,128,128]{2,1,0:T(8,128)(2,1)}) %all-gather.11.cloned.1.call-update) | async-done | bytes 2097168 | tf_op jit(solution)/shard_map/all_gather | solution.py:81
  637.2 2.5 gather_fusion.5
  639.7 4.1 fusion.3
  643.9 0.9 fusion.65
  645.2 2.8 fusion.11
  648.0 4.9 convolution_add_fusion
  653.0 2.3 fusion.63
  655.3 2.8 fusion.10
  658.1 4.9 convolution_add_fusion.1
  663.2 187.3 %all-reduce.17.cloned.1.call-done = (f32[128,128]{0,1:T(8,128)}, f32[128,128]{0,1:T(8,128)}) async-done(((f32[128,128]{0,1:T(8,128)}, f32[128,128]{0,1:T(8,128)}), (f32[128,128]{0,1:T(8,128)}, f32[128,128]{0,1:T(8,128)})) %all-reduce.17.cloned.1.call-update) | async-done | bytes 131088 | tf_op jit(solution)/shard_map/psum | solution.py:61
  850.6 1.0 copy.55
  851.5 0.9 fusion.35
  852.4 11.7 %cholesky.96 = f32[128,128]{1,0:T(8,128)S(1)} custom-call(f32[128,128]{1,0:T(8,128)S(1)} %fusion.35), custom_call_target="Cholesky" | custom-call | tf_op jit(solution)/shard_map/jit(cholesky)/cholesky | solution.py:10
  864.8 104.5 %all-reduce.15.cloned.1.call-done = f32[64,16384]{1,0:T(8,128)} async-done(((f32[64,16384]{1,0:T(8,128)}), f32[64,16384]{1,0:T(8,128)}) %all-reduce.15.cloned.1.call-update) | async-done | bytes 4194320
  969.4 1.1 constant_dynamic-slice_fusion
  970.5 0.9 reshape.389
  971.4 56.1 %reduce-scatter.5.cloned.1.call-done = f32[8,16384]{1,0:T(8,128)} async-done(((f32[64,16384]{1,0:T(8,128)}), f32[8,16384]{1,0:T(8,128)}) %reduce-scatter.5.cloned.1.call-update) | async-done | bytes 524304 | tf_op jit(solution)/shard_map/reduce_scatter | solution.py:90
  1027.5 1.9 reshape.387
  1030.1 9.8 custom-call.16
  1040.0 11.7 %cholesky.107 = f32[128,128]{1,0:T(8,128)S(1)} custom-call(f32[128,128]{1,0:T(8,128)S(1)} %fusion.31), custom_call_target="Cholesky" | custom-call | tf_op jit(solution)/shard_map/jit(cholesky)/cholesky | solution.py:10
  1053.2 10.0 custom-call.17
  1063.3 1.7 fusion.33
  1065.6 1.0 copy.61
  (95 shorter events, 19.6 us)
Async XLA Ops:
  7.2 35.1 %copy-start.12 = (s32[1,1,1,64]{3,2,1,0:T(1,128)S(1)}, s32[1,1,1,64]{3,2,1,0:T(1,128)}, u32[]{:S(2)}) copy-start(s32[1,1,1,64]{3,2,1,0:T(1,128)} %param.19) | copy-start | bytes 772
  7.2 29.1 %copy-start.11 = (s32[1,1,1,64]{3,2,1,0:T(1,128)S(1)}, s32[1,1,1,64]{3,2,1,0:T(1,128)}, u32[]{:S(2)}) copy-start(s32[1,1,1,64]{3,2,1,0:T(1,128)} %param.20) | copy-start | bytes 772
  7.2 44.5 %all-gather.5.cloned.1.call-start = ((), (), s32[]{:S(2)}) async-start(), calls=%async_computation.4 | async-start | bytes 2359296 | tf_op jit(solution)/shard_map/all_gather | solution.py:80
  9.0 97.3 %all-gather.7.cloned.1.call-start = ((), (), s32[]{:S(2)}) async-start(), calls=%async_computation.5 | async-start | bytes 2228224 | tf_op jit(solution)/shard_map/all_gather | solution.py:81
  12.1 14.0 %all-to-all-start.1 = ((s32[16,1,2]{2,1,0:T(1,128)}), s32[16,1,2]{2,1,0:T(1,128)S(1)}, u32[]{:S(2)}, u32[]{:S(2)}) async-start(s32[16,1,2]{2,1,0:T(1,128)} %copy.48), calls=%async_computation.1 | async-start | bytes 16384 | tf_op jit(solution)/shard_map/all_to_all | solution.py:51
  26.1 14.7 %all-to-all-start = ((s32[8,1,4]{2,1,0:T(1,128)}), s32[8,1,4]{2,1,0:T(1,128)S(1)}, u32[]{:S(2)}, u32[]{:S(2)}) async-start(s32[8,1,4]{2,1,0:T(1,128)} %copy.47), calls=%async_computation | async-start | bytes 8192 | tf_op jit(solution)/shard_map/all_to_all | solution.py:48
  34.3 201.6 %all-reduce.13.cloned.1.call-start = ((), (), s32[]{:S(2)}) async-start(), calls=%async_computation.10 | async-start | bytes 8388608
  55.4 53.4 %copy-start.9 = (s32[1,1,1,64,128]{4,3,2,1,0:T(8,128)S(1)}, s32[1,1,1,64,128]{4,3,2,1,0:T(8,128)}, u32[]{:S(2)}) copy-start(s32[1,1,1,64,128]{4,3,2,1,0:T(8,128)} %param.18) | copy-start | bytes 98308
  55.4 53.4 %copy-start.10 = (s32[1,1,1,64,128]{4,3,2,1,0:T(8,128)S(1)}, s32[1,1,1,64,128]{4,3,2,1,0:T(8,128)}, u32[]{:S(2)}) copy-start(s32[1,1,1,64,128]{4,3,2,1,0:T(8,128)} %param.17) | copy-start | bytes 98308
  108.9 4.1 copy-start.1
  113.0 1.4 copy-start.2
  122.1 171.6 %reduce-scatter.3.cloned.1.call-start = ((), (), s32[]{:S(2)}) async-start(), calls=%async_computation.6 | async-start | bytes 4718592 | tf_op jit(solution)/shard_map/reduce_scatter | solution.py:90
  132.3 1.0 copy-start.5
  132.3 2.2 copy-start.4
  132.3 3.9 copy-start.13
  132.3 372.9 %all-reduce.19.cloned.1.call-start = ((), (), s32[]{:S(2)}) async-start(), calls=%async_computation.13 | async-start | bytes 262144 | tf_op jit(solution)/shard_map/psum | solution.py:61
  136.1 405.1 %all-reduce.23.cloned.1.call-start = ((), (), s32[]{:S(2)}) async-start(), calls=%async_computation.15 | async-start | bytes 1572864 | tf_op jit(solution)/shard_map/psum | solution.py:92
  295.6 287.3 %all-gather.9.cloned.1.call-start = ((), (), s32[]{:S(2)}) async-start(), calls=%async_computation.7 | async-start | bytes 2359296 | tf_op jit(solution)/shard_map/all_gather | solution.py:80
  541.2 26.7 %copy-start.7 = (f32[128,512]{0,1:T(8,128)S(1)}, f32[128,512]{0,1:T(8,128)}, u32[]{:S(2)}) copy-start(f32[128,512]{0,1:T(8,128)} %get-tuple-element.18) | copy-start | bytes 786436
  544.4 92.8 %all-gather.11.cloned.1.call-start = ((), (), s32[]{:S(2)}) async-start(), calls=%async_computation.8 | async-start | bytes 2228224 | tf_op jit(solution)/shard_map/all_gather | solution.py:81
  569.5 281.0 %all-reduce.17.cloned.1.call-start = ((), (), s32[]{:S(2)}) async-start(), calls=%async_computation.12 | async-start | bytes 262144 | tf_op jit(solution)/shard_map/psum | solution.py:61
  571.8 397.6 %all-reduce.15.cloned.1.call-start = ((), (), s32[]{:S(2)}) async-start(), calls=%async_computation.11 | async-start | bytes 8388608
  639.7 4.1 copy-start
  643.9 1.4 copy-start.3
  652.9 374.5 %reduce-scatter.5.cloned.1.call-start = ((), (), s32[]{:S(2)}) async-start(), calls=%async_computation.9 | async-start | bytes 4718592 | tf_op jit(solution)/shard_map/reduce_scatter | solution.py:90
  663.0 400.3 %all-reduce.21.cloned.1.call-start = ((), (), s32[]{:S(2)}) async-start(), calls=%async_computation.14 | async-start | bytes 1572864 | tf_op jit(solution)/shard_map/psum | solution.py:92
  850.6 189.4 %copy-start.6 = (f32[128,128]{0,1:T(8,128)S(1)}, f32[128,128]{0,1:T(8,128)}, u32[]{:S(2)}) copy-start(f32[128,128]{0,1:T(8,128)} %get-tuple-element.12) | copy-start | bytes 196612
  1063.2 3.3 copy-start.8
Sparse Core Ops, SparseCore 0:
  10.4 41.2 all-gather.4
  54.7 51.5 all-gather.6
  122.2 113.6 all-reduce.12
  238.3 55.3 reduce-scatter.2
  299.1 206.1 all-reduce.18
  508.5 32.6 all-reduce.22
  544.5 38.3 all-gather.8
  585.9 51.1 all-gather.10
  642.7 207.7 all-reduce.16
  854.1 115.2 all-reduce.14
  972.1 55.3 reduce-scatter.4
  1030.7 29.7 all-reduce.20
where the time goes:
time: 1080 us
  waiting for transfers between devices  852 us (79%)
  other arithmetic  99.6 us (9%)
  matrix products  56.4 us (5%)
  local copies, waits for them, and re-layouts  34.4 us (3%)
  starting transfers between devices  17.6 us (2%)
  between operations  15.7 us (1%)
    psum x2, waiting for transfers between devices, on_device(): lax.psum((jnp.dot(users.T, users, precision=lax.Precision.HIGHEST, prefer...  396 us
    unnamed x14, waiting for transfers between devices  203 us
    reduce_scatter x2, waiting for transfers between devices, on_device(): lax.psum_scatter(user_pooled, 'tcol', scatter_dimension=0, tiled=True)  112 us
    all_gather x2, waiting for transfers between devices, on_device(): item_pool = lax.all_gather(item_half, 'trow', axis=0, tiled=True)  101 us
    another operation x12, other arithmetic, precondition(): factor = jnp.linalg.cholesky(gramian)  49.7 us
    another operation x8, other arithmetic, precondition(): return jax.scipy.linalg.cho_solve((factor, True), gradient.T).T  42.1 us
  transfers between devices with their start and end apart: 14, of which 13 were waited for; matrix products, arithmetic and copies ran while one was open for 15% of the time, Pallas kernels for 0%

commit v1 on v0

--- a/solution.py
+++ b/solution.py
@@ -1,9 +1,49 @@
+import functools
 import jax
 import jax.numpy as jnp
 from jax import lax
 from jax.sharding import PartitionSpec as P
+from jax.lax import axis_index, axis_size, ppermute
 
 ITERS = 2
+
+
+def move_the_chunk(u_in, device_axis):
+    opened = axis_size(device_axis)
+    carry_in = axis_index(device_axis)
+    known, everything, v_next = (opened, carry_in, u_in.shape[0])
+    all_blocks = []
+    for pp, nth in enumerate(u_in.shape):
+        all_blocks.append(nth * known if pp == 0 else nth)
+    back = jnp.zeros(all_blocks, u_in.dtype)
+    all_rows = lax.dynamic_update_slice_in_dim(back, u_in, everything * v_next, axis=0)
+    block_now = v_now = u_in
+    c = 1
+    while c < known // 2 + 1:
+        rack = []
+        pp = 0
+        while pp < known:
+            rack.append((pp, (pp + 1) % known))
+            pp += 1
+        block_now = ppermute(block_now, axis_name=device_axis, perm=rack)
+        all_rows = lax.dynamic_update_slice_in_dim(
+            all_rows, block_now, (everything - c) % known * v_next, axis=0
+        )
+        if 2 * c < known:
+            shelf = []
+            pp = 0
+            while pp < known:
+                shelf.append((pp, (pp - 1) % known))
+                pp = pp + 1
+            v_now = ppermute(v_now, device_axis, shelf)
+            all_rows = lax.dynamic_update_slice_in_dim(
+                all_rows, v_now, (everything + c) % known * v_next, axis=0
+            )
+        c += 1
+    return all_rows
+
+
+reach_samples_all_for = functools.partial(move_the_chunk, device_axis="trow")
 
 
 def precondition(gradient, gramian):
@@ -78,7 +118,7 @@
         user_half = users.astype(jnp.bfloat16).reshape(own_users, tile_size, rank_width)
         item_half = items.astype(jnp.bfloat16).reshape(own_items, tile_size, rank_width)
         user_pool = lax.all_gather(user_half, "tcol", axis=0, tiled=True)
-        item_pool = lax.all_gather(item_half, "trow", axis=0, tiled=True)
+        item_pool = reach_samples_all_for(item_half)
         x_tiles = user_pool[row_list]
         y_tiles = item_pool[col_list]
         predicted = jnp.einsum("tar,tbr->tab", x_tiles, y_tiles, preferred_element_type=jnp.float32)

time: 1080 us -> 1030 us (0.954)
  waiting for transfers between devices: 852 us -> 706 us
  starting transfers between devices: 17.6 us -> 83.7 us
  local copies, waits for them, and re-layouts: 34.4 us -> 58.6 us
    all_gather x2 -> x0, waiting for transfers between devices: 101 us -> none  [on_device(): item_pool = lax.all_gather(item_half, 'trow', axis=0, tiled=True)]
    ppermute x0 -> x30, starting transfers between devices: none -> 70.3 us  [the longest x14 66.4 us: move_the_chunk(): v_now = ppermute(v_now, device_axis, shelf)]
    psum x2, waiting for transfers between devices: 396 us -> 347 us  [on_device(): lax.psum((jnp.dot(users.T, users, precision=lax.Precision.HIGHEST, prefer...]
    ppermute x0 -> x30, waiting for transfers between devices: none -> 25.5 us  [the longest x16 25.5 us: move_the_chunk(): block_now = ppermute(block_now, axis_name=device_axis, perm=rack)]
    dynamic_update_slice x0 -> x32, local copies, waits for them, and re-layouts: none -> 21.1 us  [the longest x16 10.6 us: move_the_chunk(): lax.dynamic_update_slice_in_dim(all_rows, block_now, (everything - c) % k...]
    all_gather x2, waiting for transfers between devices: 20.3 us -> 0.04 us  [on_device(): user_pool = lax.all_gather(user_half, 'tcol', axis=0, tiled=True)]
    unnamed x14 -> x12, waiting for transfers between devices: 203 us -> 206 us
  transfers between devices with their start and end apart: 14 -> 42, of which waited for: 13 -> 23; matrix products, arithmetic and copies ran while one was open for 15% -> 18% of each run, Pallas kernels for 0% -> 0%
where the time goes in v1:
time: 1030 us; the launch traced here: 1020 us
  waiting for transfers between devices  706 us (69%)
  other arithmetic  98.7 us (10%)
  starting transfers between devices  83.7 us (8%)
  local copies, waits for them, and re-layouts  58.6 us (6%)
  matrix products  56.5 us (5%)
  between operations  15.8 us (2%)
    psum x2, waiting for transfers between devices, on_device(): lax.psum((jnp.dot(users.T, users, precision=lax.Precision.HIGHEST, prefer...  347 us
    unnamed x12, waiting for transfers between devices  206 us
    reduce_scatter x2, waiting for transfers between devices, on_device(): lax.psum_scatter(user_pooled, 'tcol', scatter_dimension=0, tiled=True)  112 us
    ppermute x14, starting transfers between devices, move_the_chunk(): v_now = ppermute(v_now, device_axis, shelf)  66.4 us
    another operation x12, other arithmetic, precondition(): factor = jnp.linalg.cholesky(gramian)  49.6 us
    another operation x8, other arithmetic, precondition(): return jax.scipy.linalg.cho_solve((factor, True), gradient.T).T  42 us
    ppermute x16, waiting for transfers between devices, move_the_chunk(): block_now = ppermute(block_now, axis_name=device_axis, perm=rack)  25.5 us
  transfers between devices with their start and end apart: 42, of which 23 were waited for; matrix products, arithmetic and copies ran while one was open for 18% of the time, Pallas kernels for 0%

profile of v1, /device:TPU:1, one launch (start us, length us, event | category | flops | bytes accessed | tf_op | source)
XLA Modules:
  0.0 1019.6 jit_solution(9080624345771083262)
XLA Ops:
  7.2 1.8 convert_element_type.69
  10.0 2.2 collective-permute-start
  12.2 3.7 collective-permute-start.1
  15.9 1.4 copy.66
  17.3 3.5 all-to-all-start.1
  21.0 1.3 copy.65
  23.7 1.8 broadcast.338.clone
  27.0 8.2 all-to-all-start
  37.4 4.5 all-to-all-done
  43.7 4.6 collective-permute-start.3
  50.6 4.8 collective-permute-start.5
  57.8 4.8 collective-permute-start.7
  64.9 4.8 collective-permute-start.9
  71.0 1.9 collective-permute-done.8
  72.9 5.1 collective-permute-start.11
  79.4 1.7 collective-permute-done.10
  81.1 5.1 collective-permute-start.13
  89.6 5.8 collective-permute-done.14
  96.1 2.5 gather_fusion.3
  98.7 3.7 gather_fusion.1
  102.4 4.1 fusion.1
  107.9 2.8 fusion.9
  110.7 4.9 convolution_add_fusion.2
  115.9 2.3 fusion.59
  118.2 2.8 fusion.8
  121.0 4.9 convolution_add_fusion.3
  128.1 1.6 fusion.60
  131.0 100.8 %all-reduce.13.cloned.1.call-done = f32[64,16384]{1,0:T(8,128)} async-done(((f32[64,16384]{1,0:T(8,128)}), f32[64,16384]{1,0:T(8,128)}) %all-reduce.13.cloned.1.call-update) | async-done | bytes 4194320
  233.8 55.9 %reduce-scatter.3.cloned.1.call-done = f32[8,16384]{1,0:T(8,128)} async-done(((f32[64,16384]{1,0:T(8,128)}), f32[8,16384]{1,0:T(8,128)}) %reduce-scatter.3.cloned.1.call-update) | async-done | bytes 524304 | tf_op jit(solution)/shard_map/reduce_scatter | solution.py:130
  289.7 1.9 reshape.380
  292.3 209.0 %all-reduce.19.cloned.1.call-done = (f32[128,128]{0,1:T(8,128)}, f32[128,128]{0,1:T(8,128)}) async-done(((f32[128,128]{0,1:T(8,128)}, f32[128,128]{0,1:T(8,128)}), (f32[128,128]{0,1:T(8,128)}, f32[128,128]{0,1:T(8,128)})) %all-reduce.19.cloned.1.call-update) | async-done | bytes 131088 | tf_op jit(solution)/shard_map/psum | solution.py:101
  504.1 11.7 %cholesky.74 = f32[128,128]{1,0:T(8,128)S(1)} custom-call(f32[128,128]{1,0:T(8,128)S(1)} %get-tuple-element.24), custom_call_target="Cholesky" | custom-call | tf_op jit(solution)/shard_map/jit(cholesky)/cholesky | solution.py:50
  517.0 9.8 custom-call.14
  526.8 10.4 %all-reduce.23.cloned.1.call-done = (f32[128,1024]{0,1:T(8,128)}, f32[128,512]{0,1:T(8,128)}) async-done(((f32[128,1024]{0,1:T(8,128)}, f32[128,512]{0,1:T(8,128)}), (f32[128,1024]{0,1:T(8,128)}, f32[128,512]{0,1:T(8,128)})) %all-reduce.23.cloned.1.call-update) | async-done | bytes 786448 | tf_op jit(solution)/shard_map/psum | solution.py:132
  537.3 1.7 fusion.41
  540.8 11.7 %cholesky.85 = f32[128,128]{1,0:T(8,128)S(1)} custom-call(f32[128,128]{1,0:T(8,128)S(1)} %get-tuple-element.23), custom_call_target="Cholesky" | custom-call | tf_op jit(solution)/shard_map/jit(cholesky)/cholesky | solution.py:50
  553.9 9.8 custom-call.15
  565.6 3.8 collective-permute-start.16
  571.7 1.8 broadcast.338
  575.0 4.8 collective-permute-start.18
  580.4 1.4 collective-permute-done.17
  582.5 5.0 collective-permute-start.20
  589.7 5.0 collective-permute-start.22
  596.8 5.0 collective-permute-start.24
  604.0 5.0 collective-permute-start.26
  611.2 5.0 collective-permute-start.28
  619.2 6.6 collective-permute-done.29
  626.5 2.5 gather_fusion.5
  629.1 3.7 gather_fusion.4
  632.8 4.1 fusion.3
  638.3 2.8 fusion.11
  641.1 4.9 convolution_add_fusion
  646.5 2.3 fusion.63
  648.8 2.8 fusion.10
  651.6 4.9 convolution_add_fusion.1
  656.8 138.1 %all-reduce.17.cloned.1.call-done = (f32[128,128]{0,1:T(8,128)}, f32[128,128]{0,1:T(8,128)}) async-done(((f32[128,128]{0,1:T(8,128)}, f32[128,128]{0,1:T(8,128)}), (f32[128,128]{0,1:T(8,128)}, f32[128,128]{0,1:T(8,128)})) %all-reduce.17.cloned.1.call-update) | async-done | bytes 131088 | tf_op jit(solution)/shard_map/psum | solution.py:101
  796.7 11.7 %cholesky.96 = f32[128,128]{1,0:T(8,128)S(1)} custom-call(f32[128,128]{1,0:T(8,128)S(1)} %fusion.35), custom_call_target="Cholesky" | custom-call | tf_op jit(solution)/shard_map/jit(cholesky)/cholesky | solution.py:50
  809.1 104.8 %all-reduce.15.cloned.1.call-done = f32[64,16384]{1,0:T(8,128)} async-done(((f32[64,16384]{1,0:T(8,128)}), f32[64,16384]{1,0:T(8,128)}) %all-reduce.15.cloned.1.call-update) | async-done | bytes 4194320
  915.8 56.1 %reduce-scatter.5.cloned.1.call-done = f32[8,16384]{1,0:T(8,128)} async-done(((f32[64,16384]{1,0:T(8,128)}), f32[8,16384]{1,0:T(8,128)}) %reduce-scatter.5.cloned.1.call-update) | async-done | bytes 524304 | tf_op jit(solution)/shard_map/reduce_scatter | solution.py:130
  971.9 1.9 reshape.387
  974.5 9.8 custom-call.16
  984.5 11.7 %cholesky.107 = f32[128,128]{1,0:T(8,128)S(1)} custom-call(f32[128,128]{1,0:T(8,128)S(1)} %fusion.31), custom_call_target="Cholesky" | custom-call | tf_op jit(solution)/shard_map/jit(cholesky)/cholesky | solution.py:50
  997.5 10.0 custom-call.17
  1007.6 1.7 fusion.33
  (183 shorter events, 67.0 us)
Async XLA Ops:
  7.2 91.5 %all-gather.3.cloned.1.call-start = ((), (), s32[]{:S(2)}) async-start(), calls=%async_computation.4 | async-start | bytes 2359296 | tf_op jit(solution)/shard_map/all_gather | solution.py:120
  9.0 28.3 %copy-start.11 = (s32[1,1,1,64]{3,2,1,0:T(1,128)S(1)}, s32[1,1,1,64]{3,2,1,0:T(1,128)}, u32[]{:S(2)}) copy-start(s32[1,1,1,64]{3,2,1,0:T(1,128)} %param.20) | copy-start | bytes 772
  10.0 33.4 %copy-start.12 = (s32[1,1,1,64]{3,2,1,0:T(1,128)S(1)}, s32[1,1,1,64]{3,2,1,0:T(1,128)}, u32[]{:S(2)}) copy-start(s32[1,1,1,64]{3,2,1,0:T(1,128)} %param.19) | copy-start | bytes 772
  10.0 33.4 %collective-permute-start = (bf16[4,128,128]{2,1,0:T(8,128)(2,1)S(1)}, bf16[4,128,128]{2,1,0:T(8,128)(2,1)S(1)}, u32[]{:S(2)}, u32[]{:S(2)}) collective-permute-start(bf16[4,128,128]{2,1,0:T(8,128)(2,1)S(1)} %bitcast.221), channel_id=1, source_target_pairs={{0,16},{16,32},{32,48},{48,64},{64,80},{80,96},{96,112},{112,128},... | collective-permute-start | bytes 393224 | tf_op jit(solution)/shard_map/ppermute | solution.py:28
  12.2 31.5 %collective-permute-start.1 = (bf16[4,128,128]{2,1,0:T(8,128)(2,1)S(1)}, bf16[4,128,128]{2,1,0:T(8,128)(2,1)S(1)}, u32[]{:S(2)}, u32[]{:S(2)}) collective-permute-start(bf16[4,128,128]{2,1,0:T(8,128)(2,1)S(1)} %bitcast.222), channel_id=1, source_target_pairs={{0,240},{16,0},{32,16},{48,32},{64,48},{80,64},{96,80},{112,96},{1... | collective-permute-start | bytes 393224 | tf_op jit(solution)/shard_map/ppermute | solution.py:38
  17.3 9.8 all-to-all-start.1
  27.0 14.8 %all-to-all-start = ((s32[8,1,4]{2,1,0:T(1,128)}), s32[8,1,4]{2,1,0:T(1,128)S(1)}, u32[]{:S(2)}, u32[]{:S(2)}) async-start(s32[8,1,4]{2,1,0:T(1,128)} %copy.65), calls=%async_computation | async-start | bytes 8192 | tf_op jit(solution)/shard_map/all_to_all | solution.py:88
  35.2 196.6 %all-reduce.13.cloned.1.call-start = ((), (), s32[]{:S(2)}) async-start(), calls=%async_computation.8 | async-start | bytes 8388608
  43.4 7.2 collective-permute-start.2
  43.7 6.9 collective-permute-start.3
  50.6 7.1 collective-permute-start.4
  50.6 7.1 collective-permute-start.5
  57.8 7.1 collective-permute-start.6
  57.8 7.1 collective-permute-start.7
  64.9 8.0 collective-permute-start.8
  64.9 8.0 collective-permute-start.9
  72.9 8.2 collective-permute-start.10
  72.9 8.2 collective-permute-start.11
  81.1 7.1 collective-permute-start.12
  81.1 7.8 collective-permute-start.13
  88.2 7.1 collective-permute-start.14
  98.6 3.8 copy-start.9
  98.6 3.8 copy-start.10
  102.4 4.1 copy-start.1
  106.5 1.4 copy-start.2
  115.6 174.1 %reduce-scatter.3.cloned.1.call-start = ((), (), s32[]{:S(2)}) async-start(), calls=%async_computation.5 | async-start | bytes 4718592 | tf_op jit(solution)/shard_map/reduce_scatter | solution.py:130
  125.9 0.9 copy-start.5
  125.9 2.2 copy-start.4
  125.9 3.9 copy-start.13
  125.9 375.4 %all-reduce.19.cloned.1.call-start = ((), (), s32[]{:S(2)}) async-start(), calls=%async_computation.11 | async-start | bytes 262144 | tf_op jit(solution)/shard_map/psum | solution.py:101
  129.7 407.5 %all-reduce.23.cloned.1.call-start = ((), (), s32[]{:S(2)}) async-start(), calls=%async_computation.13 | async-start | bytes 1572864 | tf_op jit(solution)/shard_map/psum | solution.py:132
  291.7 337.4 %all-gather.5.cloned.1.call-start = ((), (), s32[]{:S(2)}) async-start(), calls=%async_computation.6 | async-start | bytes 2359296 | tf_op jit(solution)/shard_map/all_gather | solution.py:120
  537.3 26.4 %copy-start.7 = (f32[128,512]{0,1:T(8,128)S(1)}, f32[128,512]{0,1:T(8,128)}, u32[]{:S(2)}) copy-start(f32[128,512]{0,1:T(8,128)} %get-tuple-element.18) | copy-start | bytes 786436
  540.4 254.4 %all-reduce.17.cloned.1.call-start = ((), (), s32[]{:S(2)}) async-start(), calls=%async_computation.10 | async-start | bytes 262144 | tf_op jit(solution)/shard_map/psum | solution.py:101
  564.6 9.6 collective-permute-start.15
  565.6 9.4 collective-permute-start.16
  574.2 339.7 %all-reduce.15.cloned.1.call-start = ((), (), s32[]{:S(2)}) async-start(), calls=%async_computation.9 | async-start | bytes 8388608
  574.2 7.6 collective-permute-start.17
  575.0 7.5 collective-permute-start.18
  581.9 7.1 collective-permute-start.19
  582.5 7.1 collective-permute-start.20
  589.0 7.1 collective-permute-start.21
  589.7 7.1 collective-permute-start.22
  596.2 7.2 collective-permute-start.23
  596.8 7.2 collective-permute-start.24
  603.3 7.2 collective-permute-start.25
  604.0 7.2 collective-permute-start.26
  610.5 7.2 collective-permute-start.27
  611.2 7.4 collective-permute-start.28
  617.7 8.1 collective-permute-start.29
  632.8 4.1 copy-start
  636.9 1.4 copy-start.3
  646.0 325.9 %reduce-scatter.5.cloned.1.call-start = ((), (), s32[]{:S(2)}) async-start(), calls=%async_computation.7 | async-start | bytes 4718592 | tf_op jit(solution)/shard_map/reduce_scatter | solution.py:130
  656.5 351.0 %all-reduce.21.cloned.1.call-start = ((), (), s32[]{:S(2)}) async-start(), calls=%async_computation.12 | async-start | bytes 1572864 | tf_op jit(solution)/shard_map/psum | solution.py:132
  794.8 189.5 %copy-start.6 = (f32[128,128]{0,1:T(8,128)S(1)}, f32[128,128]{0,1:T(8,128)}, u32[]{:S(2)}) copy-start(f32[128,128]{0,1:T(8,128)} %get-tuple-element.12) | copy-start | bytes 196612
  1007.6 3.3 copy-start.8
Sparse Core Ops, SparseCore 0:
  10.4 41.2 all-gather.2
  115.8 116.0 all-reduce.12
  234.4 55.3 reduce-scatter.2
  295.2 206.0 all-reduce.18
  504.6 32.6 all-reduce.22
  540.6 38.2 all-gather.4
  585.0 209.8 all-reduce.16
  798.6 115.2 all-reduce.14
  916.6 55.3 reduce-scatter.4
  975.2 29.5 all-reduce.20
